TPU v7x, 256 devices: a whole 4x4x8 slice. The times are simulated.
256 devices in a mesh: dp: 8 (over y, core), tensor: 32 (over x, z).
Axes of the slice: x: 4, y: 4, z: 8, core: 2. Of those that a mesh axis runs over, the one named last changes fastest.
Arguments:
- hidden_sel: bfloat16 [8, 512, 2048], P('dp', 'tensor'), may hold values from -8 to 8
- picked: int32 [8, 512], P('dp'), may hold values from 0 to 12287, as said below
- order: int32 [8, 12], P('dp'), may hold values from 0 to 11, each once within a row
- lengths: int32 [8, 3], P('dp'), may hold values from 1 to 6, 12 in all within a row
- offsets: int32 [8, 3], P('dp'), may hold values from 0 to 4095
- cache_keys: bfloat16 [8, 12288, 2048], P('dp', 'tensor'), may hold values from -64 to 64
- cache_values: bfloat16 [8, 12288, 2048], P('dp', 'tensor'), may hold values from -6 to 6
- w_qkv: bfloat16 [3, 2048, 2048], P(None, 'dp', 'tensor'), may hold values from -0.088388348 to 0.088388348
- w_out: bfloat16 [2048, 2048], P('tensor', 'dp'), may hold values from -0.125 to 0.125
- w_gate_up: bfloat16 [2, 2048, 8192], P(None, 'dp', 'tensor'), may hold values from -0.125 to 0.125
- w_down: bfloat16 [8192, 2048], P('tensor', 'dp'), may hold values from -0.0625 to 0.0625
- gains: float32 [4, 2048], replicated, may hold values from 0.5 to 1.5
Outputs:
- layer_out: bfloat16 [8, 512, 2048], P('dp', 'tensor')
- fresh_keys: bfloat16 [8, 512, 2048], P('dp', 'tensor')
Inputs may be any that keep to these rules, and one draw needn't show every extreme that they name: `picked`: distinct context rows in increasing order; the first and last rows of the context are always among them. `lengths`: they sum to 12.
All inputs are finite; a program needn't handle non-finite values.
Results may differ from a plain program's by a relative error of at most 0.04.
Values may be sent and summed in bfloat16 or wider, within the bound.
A program may use at most 64 MiB of HBM per device.

v0:
```python
import math
import jax
import jax.numpy as jnp
from jax import lax
from jax.sharding import PartitionSpec as P

HEAD_DIM = 128
CH = 1024
NCH = 12
REQS = 3
NX = 4
NZ = 8
THETA = 500000.0
EPSILON = 1e-06
NEGATIVE = -1e30
ZG = [[x * NZ + z for z in range(NZ)] for x in range(NX)]
XG = [[x * NZ + z for x in range(NX)] for z in range(NZ)]


def token_meta(rows, order_row, length_row, offset_row):
    slot_index = rows // CH
    in_span = rows % CH
    ordinal = jnp.sum(
        jnp.where(
            slot_index[:, None] == jnp.arange(NCH, dtype=jnp.int32)[None, :], order_row[None, :], 0
        ),
        axis=1,
    )
    request_end = jnp.cumsum(length_row)
    request = jnp.sum((ordinal[:, None] >= request_end[None, :]).astype(jnp.int32), axis=1)
    request_pick = request[:, None] == jnp.arange(REQS, dtype=jnp.int32)[None, :]
    request_start = jnp.sum(jnp.where(request_pick, (request_end - length_row)[None, :], 0), axis=1)
    request_shift = jnp.sum(jnp.where(request_pick, offset_row[None, :], 0), axis=1)
    position = request_shift + (ordinal - request_start) * CH + in_span
    return (request, position, in_span)


def frequencies(index_float):
    return jnp.exp(index_float * (-2.0 * math.log(THETA) / HEAD_DIM))


def rope_full(values_in, position):
    row_count = values_in.shape[0]
    half_dim = HEAD_DIM // 2
    split = values_in.reshape(row_count, -1, HEAD_DIM)
    angles = (
        position.astype(jnp.float32)[:, None]
        * frequencies(jnp.arange(half_dim, dtype=jnp.int32).astype(jnp.float32))[None, :]
    )
    cosine = jnp.cos(angles)[:, None, :]
    sine = jnp.sin(angles)[:, None, :]
    first = split[..., :half_dim]
    second = split[..., half_dim:]
    turned = jnp.concatenate(
        [first * cosine - second * sine, second * cosine + first * sine], axis=-1
    )
    return turned.reshape(row_count, -1)


def rms_scale(values_in, gain):
    return (
        values_in
        * lax.rsqrt(jnp.mean(values_in * values_in, axis=-1, keepdims=True) + EPSILON)
        * gain
    )


def swap(blocks, groups):
    return lax.all_to_all(
        blocks, "tensor", split_axis=0, concat_axis=0, axis_index_groups=groups, tiled=True
    )


def share(block, groups):
    count = len(groups[0])
    return swap(jnp.broadcast_to(block[None], (count,) + block.shape), groups)


def shards(
    hidden_sel,
    picked,
    order,
    lengths,
    offsets,
    cache_keys,
    cache_values,
    w_qkv,
    w_out,
    w_gate_up,
    w_down,
    gains,
):
    f32, bf16 = (jnp.float32, jnp.bfloat16)
    hidden = hidden_sel[0]
    meta = (order[0], lengths[0], offsets[0])
    picked_row = picked[0]
    lane = lax.axis_index("tensor")
    at_x, at_z = (lane // NZ, lane % NZ)
    own, width = hidden.shape
    sel = own * NX * NZ
    ctx = cache_keys.shape[1]
    part = width // NX
    heads = part // HEAD_DIM
    qkv_full = lax.all_gather(w_qkv, "dp", axis=1, tiled=True)
    out_full = lax.all_gather(w_out, "dp", axis=1, tiled=True)
    gate_full = lax.all_gather(w_gate_up, "dp", axis=1, tiled=True)
    down_full = lax.all_gather(w_down, "dp", axis=1, tiled=True)
    out_rows = share(out_full, ZG).reshape(part, width)
    cache = jnp.concatenate([cache_keys[0], cache_values[0]], axis=0)
    cache = swap(cache.reshape(2 * ctx, NX, part).transpose(1, 0, 2), XG)
    raw_keys = cache[:, :ctx].reshape(NX * ctx, part)
    values_c = cache[:, ctx:].reshape(NX * ctx, part)
    rows = (
        (jnp.arange(NX, dtype=jnp.int32)[:, None] * NZ + at_z) * ctx
        + jnp.arange(ctx, dtype=jnp.int32)[None, :]
    ).reshape(-1)
    c_req, c_pos, c_local = token_meta(rows, *meta)
    chosen = jnp.any(picked_row[:, None] == rows[None, :], axis=0)
    keys_c = rope_full(raw_keys.astype(f32), c_pos - c_local).astype(bf16)
    x_rows = share(hidden, ZG).reshape(NZ * own, width)
    all_rows = share(x_rows, XG).reshape(sel, width)
    proj = jnp.einsum("nd,kdc->knc", all_rows, qkv_full, preferred_element_type=f32).astype(bf16)
    cols = proj.shape[2]
    q_req, q_pos, _ = token_meta(picked_row, *meta)

    def by_z(rows_in):
        return rows_in.reshape(NX, NZ, own, -1).transpose(1, 0, 2, 3).reshape(NZ, NX * own, -1)

    def of_z(vector):
        return lax.dynamic_index_in_dim(
            vector.reshape(NX, NZ, own).transpose(1, 0, 2).reshape(NZ, NX * own),
            at_z,
            0,
            keepdims=False,
        )

    f_req, f_pos = (of_z(q_req), of_z(q_pos))
    payload = jnp.concatenate(
        [jnp.broadcast_to(proj[0][None], (NZ, sel, cols)), by_z(proj[1]), by_z(proj[2])], axis=1
    )
    got = swap(payload, ZG).transpose(1, 0, 2).reshape(-1, part).astype(f32)
    squares = jnp.sum(got[: sel + NX * own] ** 2, axis=1)
    squares = jnp.sum(share(squares, XG), axis=0)
    scale = lax.rsqrt(squares / width + EPSILON)[:, None]
    gain_x = lax.dynamic_slice_in_dim(gains, at_x * part, part, axis=1)
    query = rope_full(got[:sel] * scale[:sel] * gain_x[0], q_pos).astype(bf16)
    key_f = rope_full(got[sel : sel + NX * own] * scale[sel:] * gain_x[1], f_pos).astype(bf16)
    value_f = got[sel + NX * own :].astype(bf16)
    fresh_out = swap(key_f.reshape(NX, own, part), XG).transpose(1, 0, 2).reshape(own, width)
    all_keys = jnp.concatenate([keys_c, key_f], axis=0).reshape(-1, heads, HEAD_DIM)
    all_values = jnp.concatenate([values_c, value_f], axis=0).reshape(-1, heads, HEAD_DIM)
    k_req = jnp.concatenate([c_req, f_req])
    k_pos = jnp.concatenate([c_pos, f_pos])
    live = jnp.concatenate([jnp.logical_not(chosen), jnp.ones((NX * own,), bool)])
    scores = jnp.einsum(
        "qhd,khd->hqk", query.reshape(sel, heads, HEAD_DIM), all_keys, preferred_element_type=f32
    ) * HEAD_DIM ** (-0.5)
    usable = (q_req[:, None] == k_req[None, :]) & (k_pos[None, :] <= q_pos[:, None]) & live[None, :]
    masked = jnp.where(usable[None], scores, NEGATIVE)
    top = jnp.max(masked, axis=2)
    weights = jnp.where(usable[None], jnp.exp(masked - top[:, :, None]), 0.0)
    total = jnp.sum(weights, axis=2)
    mixed = jnp.einsum(
        "hqk,khd->qhd", weights.astype(bf16), all_values, preferred_element_type=f32
    ).reshape(sel, part)
    mixed = swap(by_z(mixed.astype(bf16)), ZG).astype(f32).reshape(NZ, NX * own, heads, HEAD_DIM)
    stats = swap(by_z(jnp.concatenate([top, total], axis=0).T), ZG)
    top, total = (stats[..., :heads], stats[..., heads:])
    factor = jnp.exp(top - jnp.max(top, axis=0))
    attn = jnp.sum(mixed * factor[..., None], axis=0) / jnp.sum(total * factor, axis=0)[..., None]
    attn = attn.reshape(NX * own, part).astype(bf16)
    y_part = jnp.dot(attn, out_rows, preferred_element_type=f32).astype(bf16)
    y = jnp.sum(swap(y_part.reshape(NX, own, width), XG).astype(f32), axis=0)
    hidden_next = (hidden.astype(f32) + rms_scale(y, gains[2])).astype(bf16)
    x_rows = share(hidden_next, ZG).reshape(NZ * own, width)
    all_next = share(x_rows, XG).reshape(sel, width)
    gate_part = jnp.dot(all_next, gate_full[0], preferred_element_type=f32)
    up_part = jnp.dot(all_next, gate_full[1], preferred_element_type=f32)
    activated = (jax.nn.silu(gate_part) * up_part).astype(bf16)
    down = jnp.dot(activated, down_full, preferred_element_type=f32).astype(bf16)
    down = jnp.sum(swap(down.reshape(NX, NZ * own, width), XG).astype(f32), axis=0).astype(bf16)
    down = jnp.sum(swap(down.reshape(NZ, own, width), ZG).astype(f32), axis=0)
    result = (hidden_next.astype(f32) + rms_scale(down, gains[3])).astype(bf16)
    return (result[None], fresh_out[None])


def solution(mesh):
    placed = (
        P("dp", "tensor", None),
        P("dp", None),
        P("dp", None),
        P("dp", None),
        P("dp", None),
        P("dp", "tensor", None),
        P("dp", "tensor", None),
        P(None, "dp", "tensor"),
        P("tensor", "dp"),
        P(None, "dp", "tensor"),
        P("tensor", "dp"),
        P(),
    )
    return jax.shard_map(
        shards,
        mesh=mesh,
        in_specs=placed,
        out_specs=(P("dp", "tensor", None), P("dp", "tensor", None)),
        check_vma=False,
    )
```

profile of v0, /device:TPU:16, one launch (start us, length us, event | category | flops | bytes accessed | tf_op | source)
XLA Modules:
  0.0 391.8 jit_solution(4341000119119259487)
XLA Ops:
  7.2 1.7 broadcast_in_dim.177
  8.8 8.5 %all-to-all-start.1 = ((bf16[8,16,2048]{2,1,0:T(8,128)(2,1)}), bf16[8,16,2048]{2,1,0:T(8,128)(2,1)S(1)}, u32[]{:S(2)}, u32[]{:S(2)}) async-start(bf16[8,16,2048]{2,1,0:T(8,128)(2,1)} %broadcast_in_dim.177), calls=%async_computation.1 | async-start | bytes 1048576 | tf_op jit(solution)/shard_map/all_to_all | solution.py:69
  18.2 2.9 concatenate.46
  22.6 2.9 concatenate.47
  28.8 6.0 %all-to-all-done.1 = bf16[8,16,2048]{2,1,0:T(8,128)(2,1)S(1)} async-done(((bf16[8,16,2048]{2,1,0:T(8,128)(2,1)}), bf16[8,16,2048]{2,1,0:T(8,128)(2,1)S(1)}, u32[]{:S(2)}, u32[]{:S(2)}) %all-to-all-start.1) | async-done | bytes 524320 | tf_op jit(solution)/shard_map/all_to_all | solution.py:69
  34.8 1.6 broadcast_in_dim.179
  36.4 4.3 %all-to-all-start.2 = ((bf16[4,128,2048]{2,1,0:T(8,128)(2,1)}), bf16[4,128,2048]{2,1,0:T(8,128)(2,1)S(1)}, u32[]{:S(2)}, u32[]{:S(2)}) async-start(bf16[4,128,2048]{2,1,0:T(8,128)(2,1)} %broadcast_in_dim.179), calls=%async_computation.2 | async-start | bytes 4194304 | tf_op jit(solution)/shard_map/all_to_all | solution.py:69
  41.7 3.7 maximum_bitcast_fusion
  45.5 21.7 %all-to-all-done.2 = bf16[4,128,2048]{2,1,0:T(8,128)(2,1)S(1)} async-done(((bf16[4,128,2048]{2,1,0:T(8,128)(2,1)}), bf16[4,128,2048]{2,1,0:T(8,128)(2,1)S(1)}, u32[]{:S(2)}, u32[]{:S(2)}) %all-to-all-start.2) | async-done | bytes 2097184 | tf_op jit(solution)/shard_map/all_to_all | solution.py:69
  68.6 3.7 all-to-all-start
  73.2 12.2 %all_gather.12 = bf16[3,2048,64]{1,2,0:T(8,128)(2,1)S(1)} all-gather(bf16[3,256,64]{1,2,0:T(8,128)(2,1)S(1)} %copy-done.13), channel_id=1, replica_groups=mesh['dp'=8,'tensor'=32] {'dp'}, dimensions={1}, use_global_device_ids=true | all-gather | bytes 884736 | tf_op jit(solution)/shard_map/all_gather | solution.py:104
  85.3 2.5 and_and_fusion
  87.8 4.3 %multiply_cosine_fusion = (f32[1536,64]{1,0:T(8,128)}, f32[1536,64]{1,0:T(8,128)}) fusion(f32[64]{0:T(128)S(1)} %multiply_exponential_fusion, f32[1536]{0:T(1024)S(1)} %get-tuple-element.35), kind=kLoop, calls=%fused_computation.33 | loop fusion | flops 98304 | bytes 792832 | tf_op jit(solution)/shard_map/cos | solution.py:50
  96.9 12.2 %all-to-all-done = bf16[4,768,512]{2,1,0:T(8,128)(2,1)S(1)} async-done(((bf16[4,768,512]{2,1,0:T(8,128)(2,1)}), bf16[4,768,512]{2,1,0:T(8,128)(2,1)S(1)}, u32[]{:S(2)}, u32[]{:S(2)}) %all-to-all-start) | async-done | bytes 3145760 | tf_op jit(solution)/shard_map/all_to_all | solution.py:69
  109.1 4.2 %all-to-all-start.3 = ((bf16[8,640,64]{1,2,0:T(8,128)(2,1)}), bf16[8,640,64]{1,2,0:T(8,128)(2,1)}, u32[]{:S(2)}, u32[]{:S(2)}) async-start(bf16[8,640,64]{1,2,0:T(8,128)(2,1)} %pad_maximum_fusion), calls=%async_computation.3 | async-start | bytes 1310720 | tf_op jit(solution)/shard_map/all_to_all | solution.py:69
  114.2 1.8 multiply_cosine_fusion.1
  116.0 2.6 fusion.70
  118.6 3.1 reshape.657
  121.7 3.5 fusion.71
  125.3 6.7 %all-to-all-done.3 = bf16[8,640,64]{1,2,0:T(8,128)(2,1)} async-done(((bf16[8,640,64]{1,2,0:T(8,128)(2,1)}), bf16[8,640,64]{1,2,0:T(8,128)(2,1)}, u32[]{:S(2)}, u32[]{:S(2)}) %all-to-all-start.3) | async-done | bytes 655392 | tf_op jit(solution)/shard_map/all_to_all | solution.py:69
  135.1 3.4 all-to-all-start.4
  138.6 4.8 %subtract_convert_fusion = (bf16[1536,4,64]{2,0,1:T(8,128)(2,1)}, bf16[1536,4,64]{2,0,1:T(8,128)(2,1)}) fusion(f32[1536,4,64]{2,1,0:T(4,128)} %get-tuple-element.18, f32[1536,4,64]{2,1,0:T(4,128)S(1)} %copy-done.1, f32[1536,64]{1,0:T(8,128)} %get-tuple-element.37, f32[1536,64]{1,0:T(8,128)} %get-tuple-element.36), kind=kLoop, calls=%fused_computation.10 | loop fusion | flops 3145728 | bytes 5505024 | tf_op jit(solution)/shard_map/convert.3
  143.4 2.4 concatenate.49
  153.7 3.6 fusion
  157.3 3.3 fusion.1
  163.2 3.3 all-to-all-start.6
  166.6 7.6 %fusion.21 = bf16[512,4,128]{0,2,1:T(8,128)(2,1)S(1)} fusion(f32[4,512,1600]{1,2,0:T(8,128)} %copy-done, f32[4,512]{1,0:T(4,128)S(1)} %get-tuple-element.42, pred[512,1600]{0,1:T(8,128)(4,1)S(1)} %copy-done.5, bf16[64,4,128]{2,0,1:T(8,128)(2,1)S(1)} %copy-done.14, bf16[1536,4,128]{2,0,1:T(8,128)(2,1)S(1)} %copy-done.7), kind=kOutput, calls=%fused_computation.27 | convolution fusion | flops 858783744 | bytes 16097280 | tf_op jit(solution)/shard_map/hqk,khd->qhd/dot_general | solution.py:163
  175.5 7.1 %all-to-all-start.5 = ((bf16[8,64,512]{2,1,0:T(8,128)(2,1)}), bf16[8,64,512]{2,1,0:T(8,128)(2,1)S(1)}, u32[]{:S(2)}, u32[]{:S(2)}) async-start(bf16[8,64,512]{2,1,0:T(8,128)(2,1)} %bitcast.33), calls=%async_computation.5 | async-start | bytes 1048576 | tf_op jit(solution)/shard_map/all_to_all | solution.py:69
  182.7 11.6 %all_gather.13 = bf16[64,2048]{1,0:T(8,128)(2,1)S(1)} all-gather(bf16[64,256]{1,0:T(8,128)(2,1)S(1)} %copy-done.15), channel_id=1, replica_groups=mesh['dp'=8,'tensor'=32] {'dp'}, dimensions={1}, use_global_device_ids=true | all-gather | bytes 294912 | tf_op jit(solution)/shard_map/all_gather | solution.py:105
  194.3 3.1 all-to-all-done.5
  197.4 1.6 broadcast_in_dim.199
  199.0 4.0 %all-to-all-start.7 = ((bf16[8,64,2048]{2,1,0:T(8,128)(2,1)}), bf16[8,64,2048]{2,1,0:T(8,128)(2,1)S(1)}, u32[]{:S(2)}, u32[]{:S(2)}) async-start(bf16[8,64,2048]{2,1,0:T(8,128)(2,1)} %broadcast_in_dim.199), calls=%async_computation.7 | async-start | bytes 4194304 | tf_op jit(solution)/shard_map/all_to_all | solution.py:69
  209.1 45.6 %all-to-all-done.7 = bf16[8,64,2048]{2,1,0:T(8,128)(2,1)S(1)} async-done(((bf16[8,64,2048]{2,1,0:T(8,128)(2,1)}), bf16[8,64,2048]{2,1,0:T(8,128)(2,1)S(1)}, u32[]{:S(2)}, u32[]{:S(2)}) %all-to-all-start.7) | async-done | bytes 2097184 | tf_op jit(solution)/shard_map/all_to_all | solution.py:69
  255.9 4.6 %all-to-all-start.8 = ((bf16[4,16,2048]{2,1,0:T(8,128)(2,1)}), bf16[4,16,2048]{2,1,0:T(8,128)(2,1)S(1)}, u32[]{:S(2)}, u32[]{:S(2)}) async-start(bf16[4,16,2048]{2,1,0:T(8,128)(2,1)} %bitcast.37), calls=%async_computation.8 | async-start | bytes 524288 | tf_op jit(solution)/shard_map/all_to_all | solution.py:69
  260.5 6.7 %all-to-all-done.8 = bf16[4,16,2048]{2,1,0:T(8,128)(2,1)S(1)} async-done(((bf16[4,16,2048]{2,1,0:T(8,128)(2,1)}), bf16[4,16,2048]{2,1,0:T(8,128)(2,1)S(1)}, u32[]{:S(2)}, u32[]{:S(2)}) %all-to-all-start.8) | async-done | bytes 262176 | tf_op jit(solution)/shard_map/all_to_all | solution.py:69
  267.5 17.7 %all_to_all.71 = bf16[8,16,2048]{2,1,0:T(8,128)(2,1)S(1)} all-to-all(bf16[8,16,2048]{2,1,0:T(8,128)(2,1)S(1)} %broadcast_in_dim.201), channel_id=1, replica_groups={{0,1,2,3,4,5,6,7},{8,9,10,11,12,13,14,15},{16,17,18,19,20,21,22,23},{24..., dimensions={0} | all-to-all | bytes 1048576 | tf_op jit(solution)/shard_map/all_to_all | solution.py:69
  285.3 1.6 broadcast_in_dim.203
  286.8 3.6 all-to-all-start.10
  291.2 21.5 %all-to-all-done.10 = bf16[4,128,2048]{2,1,0:T(8,128)(2,1)S(1)} async-done(((bf16[4,128,2048]{2,1,0:T(8,128)(2,1)}), bf16[4,128,2048]{2,1,0:T(8,128)(2,1)S(1)}, u32[]{:S(2)}, u32[]{:S(2)}) %all-to-all-start.10) | async-done | bytes 2097184 | tf_op jit(solution)/shard_map/all_to_all | solution.py:69
  312.8 1.9 fusion.28
  314.7 1.7 all-gather.5.cloned.1.call-done
  316.4 5.1 %convolution_convert_fusion = bf16[512,2048]{1,0:T(8,128)(2,1)} fusion(bf16[256,2048]{1,0:T(8,128)(2,1)} %all-gather.5.cloned.1.call-done, bf16[512,2048]{1,0:T(8,128)(2,1)S(1)} %bitcast.112, bf16[2,2048,256]{2,1,0:T(8,128)(2,1)} %all-gather.3.cloned.1.call-done, f32[512,256]{1,0:T(8,128)S(1)} %fusion.28), kind=kOutput, calls=%fused_computation.12 | convolution fusion | flops 1075576832 | bytes 6815744 | tf_op jit(solution)/shard_map/dot_general | solution.py:180
  321.6 4.2 %all-to-all-start.11 = ((bf16[4,128,2048]{2,1,0:T(8,128)(2,1)}), bf16[4,128,2048]{2,1,0:T(8,128)(2,1)S(1)}, u32[]{:S(2)}, u32[]{:S(2)}) async-start(bf16[4,128,2048]{2,1,0:T(8,128)(2,1)} %bitcast.113), calls=%async_computation.11 | async-start | bytes 4194304 | tf_op jit(solution)/shard_map/all_to_all | solution.py:69
  326.5 26.0 %all-to-all-done.11 = bf16[4,128,2048]{2,1,0:T(8,128)(2,1)S(1)} async-done(((bf16[4,128,2048]{2,1,0:T(8,128)(2,1)}), bf16[4,128,2048]{2,1,0:T(8,128)(2,1)S(1)}, u32[]{:S(2)}, u32[]{:S(2)}) %all-to-all-start.11) | async-done | bytes 2097184 | tf_op jit(solution)/shard_map/all_to_all | solution.py:69
  352.6 3.3 all-to-all-start.13
  357.2 4.3 %all-to-all-done.13 = bf16[4,16,512]{2,1,0:T(8,128)(2,1)S(1)} async-done(((bf16[4,16,512]{2,1,0:T(8,128)(2,1)}), bf16[4,16,512]{2,1,0:T(8,128)(2,1)S(1)}, u32[]{:S(2)}, u32[]{:S(2)}) %all-to-all-start.13) | async-done | bytes 65568 | tf_op jit(solution)/shard_map/all_to_all | solution.py:69
  361.4 7.0 %all-to-all-start.12 = ((bf16[8,16,2048]{2,1,0:T(8,128)(2,1)}), bf16[8,16,2048]{2,1,0:T(8,128)(2,1)S(1)}, u32[]{:S(2)}, u32[]{:S(2)}) async-start(bf16[8,16,2048]{2,1,0:T(8,128)(2,1)} %bitcast.46), calls=%async_computation.12 | async-start | bytes 1048576 | tf_op jit(solution)/shard_map/all_to_all | solution.py:69
  369.2 14.9 %all-to-all-done.12 = bf16[8,16,2048]{2,1,0:T(8,128)(2,1)S(1)} async-done(((bf16[8,16,2048]{2,1,0:T(8,128)(2,1)}), bf16[8,16,2048]{2,1,0:T(8,128)(2,1)S(1)}, u32[]{:S(2)}, u32[]{:S(2)}) %all-to-all-start.12) | async-done | bytes 524320 | tf_op jit(solution)/shard_map/all_to_all | solution.py:69
  (156 shorter events, 41.1 us)
Async XLA Ops:
  8.8 26.0 %all-to-all-start.1 = ((bf16[8,16,2048]{2,1,0:T(8,128)(2,1)}), bf16[8,16,2048]{2,1,0:T(8,128)(2,1)S(1)}, u32[]{:S(2)}, u32[]{:S(2)}) async-start(bf16[8,16,2048]{2,1,0:T(8,128)(2,1)} %broadcast_in_dim.177), calls=%async_computation.1 | async-start | bytes 1048576 | tf_op jit(solution)/shard_map/all_to_all | solution.py:69
  22.6 4.5 %copy-start.16 = (s32[1,512]{1,0:T(1,128)S(1)}, s32[1,512]{1,0:T(1,128)}, u32[]{:S(2)}) copy-start(s32[1,512]{1,0:T(1,128)} %param.13) | copy-start | bytes 6148
  22.6 4.5 %copy-start.19 = (s32[1,12]{1,0:T(1,128)S(1)}, s32[1,12]{1,0:T(1,128)}, u32[]{:S(2)}) copy-start(s32[1,12]{1,0:T(1,128)} %param.14) | copy-start | bytes 148
  22.6 4.7 %copy-start.20 = (s32[1,3]{1,0:T(1,128)S(1)}, s32[1,3]{1,0:T(1,128)}, u32[]{:S(2)}) copy-start(s32[1,3]{1,0:T(1,128)} %param.15) | copy-start | bytes 40
  22.6 4.7 %copy-start.18 = (s32[1,3]{1,0:T(1,128)S(1)}, s32[1,3]{1,0:T(1,128)}, u32[]{:S(2)}) copy-start(s32[1,3]{1,0:T(1,128)} %param.16) | copy-start | bytes 40
  36.4 30.8 %all-to-all-start.2 = ((bf16[4,128,2048]{2,1,0:T(8,128)(2,1)}), bf16[4,128,2048]{2,1,0:T(8,128)(2,1)S(1)}, u32[]{:S(2)}, u32[]{:S(2)}) async-start(bf16[4,128,2048]{2,1,0:T(8,128)(2,1)} %broadcast_in_dim.179), calls=%async_computation.2 | async-start | bytes 4194304 | tf_op jit(solution)/shard_map/all_to_all | solution.py:69
  45.5 27.7 %copy-start.13 = (bf16[3,256,64]{1,2,0:T(8,128)(2,1)S(1)}, bf16[3,256,64]{1,2,0:T(8,128)(2,1)}, u32[]{:S(2)}) copy-start(bf16[3,256,64]{1,2,0:T(8,128)(2,1)} %param.19) | copy-start | bytes 294916
  67.2 1.3 copy-start.3
  68.6 40.5 %all-to-all-start = ((bf16[4,768,512]{2,1,0:T(8,128)(2,1)}), bf16[4,768,512]{2,1,0:T(8,128)(2,1)S(1)}, u32[]{:S(2)}, u32[]{:S(2)}) async-start(bf16[4,768,512]{2,1,0:T(8,128)(2,1)} %maximum_bitcast_fusion), calls=%async_computation | async-start | bytes 6291456 | tf_op jit(solution)/shard_map/all_to_all | solution.py:69
  72.3 19.8 %copy-start.4 = (bf16[4,128,2048]{2,1,0:T(8,128)(2,1)S(1)}, bf16[4,128,2048]{2,1,0:T(8,128)(2,1)}, u32[]{:S(2)}) copy-start(bf16[4,128,2048]{2,1,0:T(8,128)(2,1)} %copy-done.3) | copy-start | bytes 6291460
  109.1 22.9 %all-to-all-start.3 = ((bf16[8,640,64]{1,2,0:T(8,128)(2,1)}), bf16[8,640,64]{1,2,0:T(8,128)(2,1)}, u32[]{:S(2)}, u32[]{:S(2)}) async-start(bf16[8,640,64]{1,2,0:T(8,128)(2,1)} %pad_maximum_fusion), calls=%async_computation.3 | async-start | bytes 1310720 | tf_op jit(solution)/shard_map/all_to_all | solution.py:69
  125.3 13.3 %copy-start.1 = (f32[1536,4,64]{2,1,0:T(4,128)S(1)}, f32[1536,4,64]{2,1,0:T(4,128)}, u32[]{:S(2)}) copy-start(f32[1536,4,64]{2,1,0:T(4,128)} %get-tuple-element.17) | copy-start | bytes 4718596
  133.2 1.2 copy-start.2
  135.1 14.5 %all-to-all-start.4 = ((f32[4,1,576]{2,1,0:T(1,128)}), f32[4,1,576]{2,1,0:T(1,128)S(1)}, u32[]{:S(2)}, u32[]{:S(2)}) async-start(f32[4,1,576]{2,1,0:T(1,128)} %broadcast_in_dim.196), calls=%async_computation.4 | async-start | bytes 20480 | tf_op jit(solution)/shard_map/all_to_all | solution.py:69
  145.7 1.4 slice-start.1
  145.7 3.9 %slice-start = ((f32[640,8,64]{0,2,1:T(8,128)}), f32[512,8,64]{0,2,1:T(8,128)S(1)}, s32[]{:S(2)}) async-start(f32[640,8,64]{0,2,1:T(8,128)} %copy-done.2), calls=%async_computation.16 | async-start | bytes 2097152 | tf_op jit(solution)/shard_map/slice | solution.py:146
  149.8 2.0 copy-start.11
  149.8 2.0 copy-start.12
  150.3 3.2 copy-start.5
  151.7 1.8 copy-start.8
  151.7 2.0 copy-start.9
  157.3 4.9 %copy-start = (f32[4,512,1600]{1,2,0:T(8,128)}, f32[4,512,1600]{1,2,0:T(8,128)S(1)}, u32[]{:S(2)}) copy-start(f32[4,512,1600]{1,2,0:T(8,128)S(1)} %get-tuple-element.43) | copy-start | bytes 39321604
  157.3 9.2 %copy-start.7 = (bf16[1536,4,128]{2,0,1:T(8,128)(2,1)S(1)}, bf16[1536,4,128]{2,0,1:T(8,128)(2,1)}, u32[]{:S(2)}) copy-start(bf16[1536,4,128]{2,0,1:T(8,128)(2,1)} %copy.128) | copy-start | bytes 4718596
  157.3 9.2 %copy-start.14 = (bf16[64,4,128]{2,0,1:T(8,128)(2,1)S(1)}, bf16[64,4,128]{2,0,1:T(8,128)(2,1)}, u32[]{:S(2)}) copy-start(bf16[64,4,128]{2,0,1:T(8,128)(2,1)} %copy.129) | copy-start | bytes 196612
  163.2 12.4 %all-to-all-start.6 = ((f32[8,1,512]{2,1,0:T(1,128)}), f32[8,1,512]{2,1,0:T(1,128)S(1)}, u32[]{:S(2)}, u32[]{:S(2)}) async-start(f32[8,1,512]{2,1,0:T(1,128)} %reshape.668), calls=%async_computation.6 | async-start | bytes 32768 | tf_op jit(solution)/shard_map/all_to_all | solution.py:69
  174.2 8.5 %copy-start.15 = (bf16[64,256]{1,0:T(8,128)(2,1)S(1)}, bf16[64,256]{1,0:T(8,128)(2,1)}, u32[]{:S(2)}) copy-start(bf16[64,256]{1,0:T(8,128)(2,1)} %param.20) | copy-start | bytes 98308
  175.5 21.9 %all-to-all-start.5 = ((bf16[8,64,512]{2,1,0:T(8,128)(2,1)}), bf16[8,64,512]{2,1,0:T(8,128)(2,1)S(1)}, u32[]{:S(2)}, u32[]{:S(2)}) async-start(bf16[8,64,512]{2,1,0:T(8,128)(2,1)} %bitcast.33), calls=%async_computation.5 | async-start | bytes 1048576 | tf_op jit(solution)/shard_map/all_to_all | solution.py:69
  197.4 1.6 copy-start.6
  199.0 55.8 %all-to-all-start.7 = ((bf16[8,64,2048]{2,1,0:T(8,128)(2,1)}), bf16[8,64,2048]{2,1,0:T(8,128)(2,1)S(1)}, u32[]{:S(2)}, u32[]{:S(2)}) async-start(bf16[8,64,2048]{2,1,0:T(8,128)(2,1)} %broadcast_in_dim.199), calls=%async_computation.7 | async-start | bytes 4194304 | tf_op jit(solution)/shard_map/all_to_all | solution.py:69
  203.0 88.2 %all-gather.3.cloned.1.call-start = ((), (), s32[]{:S(2)}) async-start(), calls=%async_computation.14 | async-start | bytes 2359296 | tf_op jit(solution)/shard_map/all_gather | solution.py:106
  205.9 54.6 %copy-start.17 = (f32[4,2048]{1,0:T(4,128)S(1)}, f32[4,2048]{1,0:T(4,128)}, u32[]{:S(2)}) copy-start(f32[4,2048]{1,0:T(4,128)} %param.23) | copy-start | bytes 98308
  207.3 60.1 %copy-start.10 = (bf16[1,16,2048]{2,1,0:T(8,128)(2,1)S(1)}, bf16[1,16,2048]{2,1,0:T(8,128)(2,1)}, u32[]{:S(2)}) copy-start(bf16[1,16,2048]{2,1,0:T(8,128)(2,1)} %param.12) | copy-start | bytes 196612
  255.9 11.3 %all-to-all-start.8 = ((bf16[4,16,2048]{2,1,0:T(8,128)(2,1)}), bf16[4,16,2048]{2,1,0:T(8,128)(2,1)S(1)}, u32[]{:S(2)}, u32[]{:S(2)}) async-start(bf16[4,16,2048]{2,1,0:T(8,128)(2,1)} %bitcast.37), calls=%async_computation.8 | async-start | bytes 524288 | tf_op jit(solution)/shard_map/all_to_all | solution.py:69
  286.8 25.9 %all-to-all-start.10 = ((bf16[4,128,2048]{2,1,0:T(8,128)(2,1)}), bf16[4,128,2048]{2,1,0:T(8,128)(2,1)S(1)}, u32[]{:S(2)}, u32[]{:S(2)}) async-start(bf16[4,128,2048]{2,1,0:T(8,128)(2,1)} %broadcast_in_dim.203), calls=%async_computation.10 | async-start | bytes 4194304 | tf_op jit(solution)/shard_map/all_to_all | solution.py:69
  290.4 26.0 %all-gather.5.cloned.1.call-start = ((), (), s32[]{:S(2)}) async-start(), calls=%async_computation.15 | async-start | bytes 1179648 | tf_op jit(solution)/shard_map/all_gather | solution.py:107
  321.6 31.0 %all-to-all-start.11 = ((bf16[4,128,2048]{2,1,0:T(8,128)(2,1)}), bf16[4,128,2048]{2,1,0:T(8,128)(2,1)S(1)}, u32[]{:S(2)}, u32[]{:S(2)}) async-start(bf16[4,128,2048]{2,1,0:T(8,128)(2,1)} %bitcast.113), calls=%async_computation.11 | async-start | bytes 4194304 | tf_op jit(solution)/shard_map/all_to_all | solution.py:69
  352.6 8.9 %all-to-all-start.13 = ((bf16[4,16,512]{2,1,0:T(8,128)(2,1)}), bf16[4,16,512]{2,1,0:T(8,128)(2,1)S(1)}, u32[]{:S(2)}, u32[]{:S(2)}) async-start(bf16[4,16,512]{2,1,0:T(8,128)(2,1)} %convert_element_type.166), calls=%async_computation.13 | async-start | bytes 131072 | tf_op jit(solution)/shard_map/all_to_all | solution.py:69
  361.4 22.6 %all-to-all-start.12 = ((bf16[8,16,2048]{2,1,0:T(8,128)(2,1)}), bf16[8,16,2048]{2,1,0:T(8,128)(2,1)S(1)}, u32[]{:S(2)}, u32[]{:S(2)}) async-start(bf16[8,16,2048]{2,1,0:T(8,128)(2,1)} %bitcast.46), calls=%async_computation.12 | async-start | bytes 1048576 | tf_op jit(solution)/shard_map/all_to_all | solution.py:69
Sparse Core Ops, SparseCore 0:
  205.7 29.5 all-gather.2
  293.1 23.2 all-gather.4
where the time goes:
time: 394 us; the launch traced here: 392 us
  waiting for transfers between devices  172 us (44%)
  starting transfers between devices  61.6 us (16%)
  local copies, waits for them, and re-layouts  45.3 us (11%)
  blocking collectives  41.5 us (11%)
  other arithmetic  36.6 us (9%)
  matrix products  20.3 us (5%)
  between operations  14.8 us (4%)
    all_to_all x13, waiting for transfers between devices, swap(): lax.all_to_all(blocks, 'tensor', split_axis=0, concat_axis=0, axis_index_...  169 us
    all_to_all x13, starting transfers between devices, swap(): lax.all_to_all(blocks, 'tensor', split_axis=0, concat_axis=0, axis_index_...  61.3 us
    all_to_all x1, blocking collectives, swap(): lax.all_to_all(blocks, 'tensor', split_axis=0, concat_axis=0, axis_index_...  17.7 us
    all_gather x1, blocking collectives, shards(): qkv_full = lax.all_gather(w_qkv, 'dp', axis=1, tiled=True)  12.2 us
    all_gather x1, blocking collectives, shards(): out_full = lax.all_gather(w_out, 'dp', axis=1, tiled=True)  11.6 us
    concatenate x4, local copies, waits for them, and re-layouts, shards(): cache = jnp.concatenate([cache_keys[0], cache_values[0]], axis=0)  8.78 us
  transfers between devices with their start and end apart: 15, of which 12 were waited for; matrix products, arithmetic and copies ran while one was open for 19% of the time, Pallas kernels for 0%

commit v1 on v0

--- a/solution.py
+++ b/solution.py
@@ -102,7 +102,9 @@
     part = width // NX
     heads = part // HEAD_DIM
     qkv_full = lax.all_gather(w_qkv, "dp", axis=1, tiled=True)
-    out_full = lax.all_gather(w_out, "dp", axis=1, tiled=True)
+    out_full = jnp.concatenate(
+        lax.all_to_all(jnp.stack([w_out] * lax.axis_size("dp")), "dp", 0, 0), axis=1
+    )
     gate_full = lax.all_gather(w_gate_up, "dp", axis=1, tiled=True)
     down_full = lax.all_gather(w_down, "dp", axis=1, tiled=True)
     out_rows = share(out_full, ZG).reshape(part, width)

time: 394 us -> 401 us (1.018)
  waiting for transfers between devices: 172 us -> 181 us
  blocking collectives: 41.5 us -> 33.4 us
    all_gather x1 -> x0, blocking collectives: 11.6 us -> none  [shards(): out_full = lax.all_gather(w_out, 'dp', axis=1, tiled=True)]
    all_to_all x13, waiting for transfers between devices: 169 us -> 180 us  [swap(): lax.all_to_all(blocks, 'tensor', split_axis=0, concat_axis=0, axis_index_...]
    all_to_all x0 -> x1, starting transfers between devices: none -> 4.8 us  [shards(): lax.all_to_all(jnp.stack([w_out] * lax.axis_size('dp')), 'dp', 0, 0)]
    broadcast_in_dim x6 -> x7, local copies, waits for them, and re-layouts: 7.07 us -> 8.06 us  [share(): return swap(jnp.broadcast_to(block[None], (count,) + block.shape), groups)]
  transfers between devices with their start and end apart: 15 -> 16, of which waited for: 12 -> 11; matrix products, arithmetic and copies ran while one was open for 19% -> 22% of each run, Pallas kernels for 0% -> 0%
where the time goes in v1:
time: 401 us; the launch traced here: 399 us
  waiting for transfers between devices  181 us (45%)
  starting transfers between devices  65.5 us (16%)
  local copies, waits for them, and re-layouts  47 us (12%)
  other arithmetic  36.6 us (9%)
  blocking collectives  33.4 us (8%)
  matrix products  20.3 us (5%)
  between operations  14.8 us (4%)
    all_to_all x13, waiting for transfers between devices, swap(): lax.all_to_all(blocks, 'tensor', split_axis=0, concat_axis=0, axis_index_...  180 us
    all_to_all x13, starting transfers between devices, swap(): lax.all_to_all(blocks, 'tensor', split_axis=0, concat_axis=0, axis_index_...  60.6 us
    all_to_all x1, blocking collectives, swap(): lax.all_to_all(blocks, 'tensor', split_axis=0, concat_axis=0, axis_index_...  21.2 us
    all_gather x1, blocking collectives, shards(): qkv_full = lax.all_gather(w_qkv, 'dp', axis=1, tiled=True)  12.2 us
    concatenate x4, local copies, waits for them, and re-layouts, shards(): cache = jnp.concatenate([cache_keys[0], cache_values[0]], axis=0)  8.79 us
    broadcast_in_dim x7, local copies, waits for them, and re-layouts, share(): return swap(jnp.broadcast_to(block[None], (count,) + block.shape), groups)  8.06 us
  transfers between devices with their start and end apart: 16, of which 11 were waited for; matrix products, arithmetic and copies ran while one was open for 22% of the time, Pallas kernels for 0%

profile of v1, /device:TPU:16, one launch (start us, length us, event | category | flops | bytes accessed | tf_op | source)
XLA Modules:
  0.0 398.6 jit_solution(5034796336624501113)
XLA Ops:
  7.2 1.7 broadcast_in_dim.178
  8.8 8.5 %all-to-all-start.1 = ((bf16[8,16,2048]{2,1,0:T(8,128)(2,1)}), bf16[8,16,2048]{2,1,0:T(8,128)(2,1)S(1)}, u32[]{:S(2)}, u32[]{:S(2)}) async-start(bf16[8,16,2048]{2,1,0:T(8,128)(2,1)} %broadcast_in_dim.178), calls=%async_computation.1 | async-start | bytes 1048576 | tf_op jit(solution)/shard_map/all_to_all | solution.py:69
  18.2 2.9 concatenate.46
  22.6 2.9 concatenate.47
  28.8 6.0 %all-to-all-done.1 = bf16[8,16,2048]{2,1,0:T(8,128)(2,1)S(1)} async-done(((bf16[8,16,2048]{2,1,0:T(8,128)(2,1)}), bf16[8,16,2048]{2,1,0:T(8,128)(2,1)S(1)}, u32[]{:S(2)}, u32[]{:S(2)}) %all-to-all-start.1) | async-done | bytes 524320 | tf_op jit(solution)/shard_map/all_to_all | solution.py:69
  34.8 1.6 broadcast_in_dim.180
  36.4 4.3 %all-to-all-start.2 = ((bf16[4,128,2048]{2,1,0:T(8,128)(2,1)}), bf16[4,128,2048]{2,1,0:T(8,128)(2,1)S(1)}, u32[]{:S(2)}, u32[]{:S(2)}) async-start(bf16[4,128,2048]{2,1,0:T(8,128)(2,1)} %broadcast_in_dim.180), calls=%async_computation.2 | async-start | bytes 4194304 | tf_op jit(solution)/shard_map/all_to_all | solution.py:69
  41.7 3.7 maximum_bitcast_fusion
  45.5 21.7 %all-to-all-done.2 = bf16[4,128,2048]{2,1,0:T(8,128)(2,1)S(1)} async-done(((bf16[4,128,2048]{2,1,0:T(8,128)(2,1)}), bf16[4,128,2048]{2,1,0:T(8,128)(2,1)S(1)}, u32[]{:S(2)}, u32[]{:S(2)}) %all-to-all-start.2) | async-done | bytes 2097184 | tf_op jit(solution)/shard_map/all_to_all | solution.py:69
  68.6 3.7 all-to-all-start
  73.2 12.2 %all_gather.9 = bf16[3,2048,64]{1,2,0:T(8,128)(2,1)S(1)} all-gather(bf16[3,256,64]{1,2,0:T(8,128)(2,1)S(1)} %copy-done.13), channel_id=1, replica_groups=mesh['dp'=8,'tensor'=32] {'dp'}, dimensions={1}, use_global_device_ids=true | all-gather | bytes 884736 | tf_op jit(solution)/shard_map/all_gather | solution.py:104
  85.4 2.5 and_and_fusion
  87.8 4.3 %multiply_cosine_fusion = (f32[1536,64]{1,0:T(8,128)}, f32[1536,64]{1,0:T(8,128)}) fusion(f32[64]{0:T(128)S(1)} %multiply_exponential_fusion, f32[1536]{0:T(1024)S(1)} %get-tuple-element.35), kind=kLoop, calls=%fused_computation.33 | loop fusion | flops 98304 | bytes 792832 | tf_op jit(solution)/shard_map/cos | solution.py:50
  96.9 12.2 %all-to-all-done = bf16[4,768,512]{2,1,0:T(8,128)(2,1)S(1)} async-done(((bf16[4,768,512]{2,1,0:T(8,128)(2,1)}), bf16[4,768,512]{2,1,0:T(8,128)(2,1)S(1)}, u32[]{:S(2)}, u32[]{:S(2)}) %all-to-all-start) | async-done | bytes 3145760 | tf_op jit(solution)/shard_map/all_to_all | solution.py:69
  109.1 4.2 %all-to-all-start.3 = ((bf16[8,640,64]{1,2,0:T(8,128)(2,1)}), bf16[8,640,64]{1,2,0:T(8,128)(2,1)}, u32[]{:S(2)}, u32[]{:S(2)}) async-start(bf16[8,640,64]{1,2,0:T(8,128)(2,1)} %pad_maximum_fusion), calls=%async_computation.3 | async-start | bytes 1310720 | tf_op jit(solution)/shard_map/all_to_all | solution.py:69
  114.2 1.8 multiply_cosine_fusion.1
  116.0 2.6 fusion.70
  118.6 3.1 reshape.663
  121.7 3.5 fusion.71
  125.3 6.7 %all-to-all-done.3 = bf16[8,640,64]{1,2,0:T(8,128)(2,1)} async-done(((bf16[8,640,64]{1,2,0:T(8,128)(2,1)}), bf16[8,640,64]{1,2,0:T(8,128)(2,1)}, u32[]{:S(2)}, u32[]{:S(2)}) %all-to-all-start.3) | async-done | bytes 655392 | tf_op jit(solution)/shard_map/all_to_all | solution.py:69
  135.1 3.3 all-to-all-start.4
  138.4 4.8 %subtract_convert_fusion = (bf16[1536,4,64]{2,0,1:T(8,128)(2,1)}, bf16[1536,4,64]{2,0,1:T(8,128)(2,1)}) fusion(f32[1536,4,64]{2,1,0:T(4,128)} %get-tuple-element.18, f32[1536,4,64]{2,1,0:T(4,128)S(1)} %copy-done.1, f32[1536,64]{1,0:T(8,128)} %get-tuple-element.37, f32[1536,64]{1,0:T(8,128)} %get-tuple-element.36), kind=kLoop, calls=%fused_computation.10 | loop fusion | flops 3145728 | bytes 5505024 | tf_op jit(solution)/shard_map/convert.3
  143.2 2.4 concatenate.49
  150.2 4.8 %all-to-all-start.7 = ((bf16[8,64,256]{2,1,0:T(8,128)(2,1)}), bf16[8,64,256]{2,1,0:T(8,128)(2,1)}, u32[]{:S(2)}, u32[]{:S(2)}) async-start(bf16[8,64,256]{2,1,0:T(8,128)(2,1)} %stack.2), calls=%async_computation.7 | async-start | bytes 524288 | tf_op jit(solution)/shard_map/all_to_all | solution.py:106
  159.1 3.6 fusion
  162.7 3.3 fusion.1
  166.0 1.6 copy-done
  168.6 3.3 all-to-all-start.6
  171.9 7.6 %fusion.21 = bf16[512,4,128]{0,2,1:T(8,128)(2,1)S(1)} fusion(f32[4,512,1600]{1,2,0:T(8,128)} %copy-done, f32[4,512]{1,0:T(4,128)S(1)} %get-tuple-element.42, pred[512,1600]{0,1:T(8,128)(4,1)S(1)} %copy-done.5, bf16[64,4,128]{2,0,1:T(8,128)(2,1)S(1)} %copy-done.14, bf16[1536,4,128]{2,0,1:T(8,128)(2,1)S(1)} %copy-done.7), kind=kOutput, calls=%fused_computation.27 | convolution fusion | flops 858783744 | bytes 16097280 | tf_op jit(solution)/shard_map/hqk,khd->qhd/dot_general | solution.py:165
  180.9 7.1 %all-to-all-start.5 = ((bf16[8,64,512]{2,1,0:T(8,128)(2,1)}), bf16[8,64,512]{2,1,0:T(8,128)(2,1)S(1)}, u32[]{:S(2)}, u32[]{:S(2)}) async-start(bf16[8,64,512]{2,1,0:T(8,128)(2,1)} %bitcast.33), calls=%async_computation.5 | async-start | bytes 1048576 | tf_op jit(solution)/shard_map/all_to_all | solution.py:69
  189.0 16.6 %all-to-all-done.5 = bf16[8,64,512]{2,1,0:T(8,128)(2,1)S(1)} async-done(((bf16[8,64,512]{2,1,0:T(8,128)(2,1)}), bf16[8,64,512]{2,1,0:T(8,128)(2,1)S(1)}, u32[]{:S(2)}, u32[]{:S(2)}) %all-to-all-start.5) | async-done | bytes 524320 | tf_op jit(solution)/shard_map/all_to_all | solution.py:69
  205.6 1.6 broadcast_in_dim.201
  207.1 3.6 all-to-all-start.8
  216.8 42.0 %all-to-all-done.8 = bf16[8,64,2048]{2,1,0:T(8,128)(2,1)S(1)} async-done(((bf16[8,64,2048]{2,1,0:T(8,128)(2,1)}), bf16[8,64,2048]{2,1,0:T(8,128)(2,1)S(1)}, u32[]{:S(2)}, u32[]{:S(2)}) %all-to-all-start.8) | async-done | bytes 2097184 | tf_op jit(solution)/shard_map/all_to_all | solution.py:69
  259.9 4.8 %all-to-all-start.9 = ((bf16[4,16,2048]{2,1,0:T(8,128)(2,1)}), bf16[4,16,2048]{2,1,0:T(8,128)(2,1)S(1)}, u32[]{:S(2)}, u32[]{:S(2)}) async-start(bf16[4,16,2048]{2,1,0:T(8,128)(2,1)} %bitcast.38), calls=%async_computation.9 | async-start | bytes 524288 | tf_op jit(solution)/shard_map/all_to_all | solution.py:69
  264.7 6.8 %all-to-all-done.9 = bf16[4,16,2048]{2,1,0:T(8,128)(2,1)S(1)} async-done(((bf16[4,16,2048]{2,1,0:T(8,128)(2,1)}), bf16[4,16,2048]{2,1,0:T(8,128)(2,1)S(1)}, u32[]{:S(2)}, u32[]{:S(2)}) %all-to-all-start.9) | async-done | bytes 262176 | tf_op jit(solution)/shard_map/all_to_all | solution.py:69
  271.9 21.2 %all_to_all.76 = bf16[8,16,2048]{2,1,0:T(8,128)(2,1)S(1)} all-to-all(bf16[8,16,2048]{2,1,0:T(8,128)(2,1)S(1)} %broadcast_in_dim.203), channel_id=1, replica_groups={{0,1,2,3,4,5,6,7},{8,9,10,11,12,13,14,15},{16,17,18,19,20,21,22,23},{24..., dimensions={0} | all-to-all | bytes 1048576 | tf_op jit(solution)/shard_map/all_to_all | solution.py:69
  293.1 1.6 broadcast_in_dim.205
  294.6 3.6 all-to-all-start.11
  299.0 22.5 %all-to-all-done.11 = bf16[4,128,2048]{2,1,0:T(8,128)(2,1)S(1)} async-done(((bf16[4,128,2048]{2,1,0:T(8,128)(2,1)}), bf16[4,128,2048]{2,1,0:T(8,128)(2,1)S(1)}, u32[]{:S(2)}, u32[]{:S(2)}) %all-to-all-start.11) | async-done | bytes 2097184 | tf_op jit(solution)/shard_map/all_to_all | solution.py:69
  321.5 1.9 fusion.28
  323.5 5.2 %convolution_convert_fusion = bf16[512,2048]{1,0:T(8,128)(2,1)} fusion(bf16[256,2048]{1,0:T(8,128)(2,1)} %all-gather.5.cloned.1.call-done, bf16[512,2048]{1,0:T(8,128)(2,1)S(1)} %bitcast.115, bf16[2,2048,256]{2,1,0:T(8,128)(2,1)} %all-gather.3.cloned.1.call-done, f32[512,256]{1,0:T(8,128)S(1)} %fusion.28), kind=kOutput, calls=%fused_computation.12 | convolution fusion | flops 1075576832 | bytes 6815744 | tf_op jit(solution)/shard_map/dot_general | solution.py:182
  328.6 4.0 all-to-all-start.12
  333.3 26.0 %all-to-all-done.12 = bf16[4,128,2048]{2,1,0:T(8,128)(2,1)S(1)} async-done(((bf16[4,128,2048]{2,1,0:T(8,128)(2,1)}), bf16[4,128,2048]{2,1,0:T(8,128)(2,1)S(1)}, u32[]{:S(2)}, u32[]{:S(2)}) %all-to-all-start.12) | async-done | bytes 2097184 | tf_op jit(solution)/shard_map/all_to_all | solution.py:69
  359.3 3.3 all-to-all-start.14
  363.9 4.3 %all-to-all-done.14 = bf16[4,16,512]{2,1,0:T(8,128)(2,1)S(1)} async-done(((bf16[4,16,512]{2,1,0:T(8,128)(2,1)}), bf16[4,16,512]{2,1,0:T(8,128)(2,1)S(1)}, u32[]{:S(2)}, u32[]{:S(2)}) %all-to-all-start.14) | async-done | bytes 65568 | tf_op jit(solution)/shard_map/all_to_all | solution.py:69
  368.2 7.0 %all-to-all-start.13 = ((bf16[8,16,2048]{2,1,0:T(8,128)(2,1)}), bf16[8,16,2048]{2,1,0:T(8,128)(2,1)S(1)}, u32[]{:S(2)}, u32[]{:S(2)}) async-start(bf16[8,16,2048]{2,1,0:T(8,128)(2,1)} %bitcast.47), calls=%async_computation.13 | async-start | bytes 1048576 | tf_op jit(solution)/shard_map/all_to_all | solution.py:69
  376.0 14.9 %all-to-all-done.13 = bf16[8,16,2048]{2,1,0:T(8,128)(2,1)S(1)} async-done(((bf16[8,16,2048]{2,1,0:T(8,128)(2,1)}), bf16[8,16,2048]{2,1,0:T(8,128)(2,1)S(1)}, u32[]{:S(2)}, u32[]{:S(2)}) %all-to-all-start.13) | async-done | bytes 524320 | tf_op jit(solution)/shard_map/all_to_all | solution.py:69
  (159 shorter events, 41.2 us)
Async XLA Ops:
  8.8 26.0 %all-to-all-start.1 = ((bf16[8,16,2048]{2,1,0:T(8,128)(2,1)}), bf16[8,16,2048]{2,1,0:T(8,128)(2,1)S(1)}, u32[]{:S(2)}, u32[]{:S(2)}) async-start(bf16[8,16,2048]{2,1,0:T(8,128)(2,1)} %broadcast_in_dim.178), calls=%async_computation.1 | async-start | bytes 1048576 | tf_op jit(solution)/shard_map/all_to_all | solution.py:69
  22.6 4.5 %copy-start.16 = (s32[1,512]{1,0:T(1,128)S(1)}, s32[1,512]{1,0:T(1,128)}, u32[]{:S(2)}) copy-start(s32[1,512]{1,0:T(1,128)} %param.13) | copy-start | bytes 6148
  22.6 4.5 %copy-start.19 = (s32[1,12]{1,0:T(1,128)S(1)}, s32[1,12]{1,0:T(1,128)}, u32[]{:S(2)}) copy-start(s32[1,12]{1,0:T(1,128)} %param.14) | copy-start | bytes 148
  22.6 4.7 %copy-start.20 = (s32[1,3]{1,0:T(1,128)S(1)}, s32[1,3]{1,0:T(1,128)}, u32[]{:S(2)}) copy-start(s32[1,3]{1,0:T(1,128)} %param.15) | copy-start | bytes 40
  22.6 4.8 %copy-start.18 = (s32[1,3]{1,0:T(1,128)S(1)}, s32[1,3]{1,0:T(1,128)}, u32[]{:S(2)}) copy-start(s32[1,3]{1,0:T(1,128)} %param.16) | copy-start | bytes 40
  36.4 30.8 %all-to-all-start.2 = ((bf16[4,128,2048]{2,1,0:T(8,128)(2,1)}), bf16[4,128,2048]{2,1,0:T(8,128)(2,1)S(1)}, u32[]{:S(2)}, u32[]{:S(2)}) async-start(bf16[4,128,2048]{2,1,0:T(8,128)(2,1)} %broadcast_in_dim.180), calls=%async_computation.2 | async-start | bytes 4194304 | tf_op jit(solution)/shard_map/all_to_all | solution.py:69
  45.5 27.7 %copy-start.13 = (bf16[3,256,64]{1,2,0:T(8,128)(2,1)S(1)}, bf16[3,256,64]{1,2,0:T(8,128)(2,1)}, u32[]{:S(2)}) copy-start(bf16[3,256,64]{1,2,0:T(8,128)(2,1)} %param.19) | copy-start | bytes 294916
  67.2 1.4 copy-start.3
  68.6 40.5 %all-to-all-start = ((bf16[4,768,512]{2,1,0:T(8,128)(2,1)}), bf16[4,768,512]{2,1,0:T(8,128)(2,1)S(1)}, u32[]{:S(2)}, u32[]{:S(2)}) async-start(bf16[4,768,512]{2,1,0:T(8,128)(2,1)} %maximum_bitcast_fusion), calls=%async_computation | async-start | bytes 6291456 | tf_op jit(solution)/shard_map/all_to_all | solution.py:69
  72.3 19.8 %copy-start.4 = (bf16[4,128,2048]{2,1,0:T(8,128)(2,1)S(1)}, bf16[4,128,2048]{2,1,0:T(8,128)(2,1)}, u32[]{:S(2)}) copy-start(bf16[4,128,2048]{2,1,0:T(8,128)(2,1)} %copy-done.3) | copy-start | bytes 6291460
  109.1 22.9 %all-to-all-start.3 = ((bf16[8,640,64]{1,2,0:T(8,128)(2,1)}), bf16[8,640,64]{1,2,0:T(8,128)(2,1)}, u32[]{:S(2)}, u32[]{:S(2)}) async-start(bf16[8,640,64]{1,2,0:T(8,128)(2,1)} %pad_maximum_fusion), calls=%async_computation.3 | async-start | bytes 1310720 | tf_op jit(solution)/shard_map/all_to_all | solution.py:69
  125.3 13.1 %copy-start.1 = (f32[1536,4,64]{2,1,0:T(4,128)S(1)}, f32[1536,4,64]{2,1,0:T(4,128)}, u32[]{:S(2)}) copy-start(f32[1536,4,64]{2,1,0:T(4,128)} %get-tuple-element.17) | copy-start | bytes 4718596
  133.2 1.1 copy-start.2
  135.1 14.3 %all-to-all-start.4 = ((f32[4,1,576]{2,1,0:T(1,128)}), f32[4,1,576]{2,1,0:T(1,128)S(1)}, u32[]{:S(2)}, u32[]{:S(2)}) async-start(f32[4,1,576]{2,1,0:T(1,128)} %broadcast_in_dim.197), calls=%async_computation.4 | async-start | bytes 20480 | tf_op jit(solution)/shard_map/all_to_all | solution.py:69
  145.5 1.4 slice-start.1
  145.6 3.9 copy-start.15
  145.6 9.5 %slice-start = ((f32[640,8,64]{0,2,1:T(8,128)}), f32[512,8,64]{0,2,1:T(8,128)S(1)}, s32[]{:S(2)}) async-start(f32[640,8,64]{0,2,1:T(8,128)} %copy-done.2), calls=%async_computation.17 | async-start | bytes 2097152 | tf_op jit(solution)/shard_map/slice | solution.py:148
  150.2 18.4 %all-to-all-start.7 = ((bf16[8,64,256]{2,1,0:T(8,128)(2,1)}), bf16[8,64,256]{2,1,0:T(8,128)(2,1)}, u32[]{:S(2)}, u32[]{:S(2)}) async-start(bf16[8,64,256]{2,1,0:T(8,128)(2,1)} %stack.2), calls=%async_computation.7 | async-start | bytes 524288 | tf_op jit(solution)/shard_map/all_to_all | solution.py:106
  155.2 2.0 copy-start.11
  155.2 2.0 copy-start.12
  155.7 3.2 copy-start.5
  157.0 1.8 copy-start.8
  157.1 2.0 copy-start.9
  162.7 4.9 %copy-start = (f32[4,512,1600]{1,2,0:T(8,128)}, f32[4,512,1600]{1,2,0:T(8,128)S(1)}, u32[]{:S(2)}) copy-start(f32[4,512,1600]{1,2,0:T(8,128)S(1)} %get-tuple-element.43) | copy-start | bytes 39321604
  162.7 9.2 %copy-start.7 = (bf16[1536,4,128]{2,0,1:T(8,128)(2,1)S(1)}, bf16[1536,4,128]{2,0,1:T(8,128)(2,1)}, u32[]{:S(2)}) copy-start(bf16[1536,4,128]{2,0,1:T(8,128)(2,1)} %copy.130) | copy-start | bytes 4718596
  162.7 9.2 %copy-start.14 = (bf16[64,4,128]{2,0,1:T(8,128)(2,1)S(1)}, bf16[64,4,128]{2,0,1:T(8,128)(2,1)}, u32[]{:S(2)}) copy-start(bf16[64,4,128]{2,0,1:T(8,128)(2,1)} %copy.131) | copy-start | bytes 196612
  168.6 12.3 %all-to-all-start.6 = ((f32[8,1,512]{2,1,0:T(1,128)}), f32[8,1,512]{2,1,0:T(1,128)S(1)}, u32[]{:S(2)}, u32[]{:S(2)}) async-start(f32[8,1,512]{2,1,0:T(1,128)} %reshape.674), calls=%async_computation.6 | async-start | bytes 32768 | tf_op jit(solution)/shard_map/all_to_all | solution.py:69
  180.9 24.7 %all-to-all-start.5 = ((bf16[8,64,512]{2,1,0:T(8,128)(2,1)}), bf16[8,64,512]{2,1,0:T(8,128)(2,1)S(1)}, u32[]{:S(2)}, u32[]{:S(2)}) async-start(bf16[8,64,512]{2,1,0:T(8,128)(2,1)} %bitcast.33), calls=%async_computation.5 | async-start | bytes 1048576 | tf_op jit(solution)/shard_map/all_to_all | solution.py:69
  205.6 1.6 copy-start.6
  207.1 51.6 %all-to-all-start.8 = ((bf16[8,64,2048]{2,1,0:T(8,128)(2,1)}), bf16[8,64,2048]{2,1,0:T(8,128)(2,1)S(1)}, u32[]{:S(2)}, u32[]{:S(2)}) async-start(bf16[8,64,2048]{2,1,0:T(8,128)(2,1)} %broadcast_in_dim.201), calls=%async_computation.8 | async-start | bytes 4194304 | tf_op jit(solution)/shard_map/all_to_all | solution.py:69
  210.7 88.3 %all-gather.3.cloned.1.call-start = ((), (), s32[]{:S(2)}) async-start(), calls=%async_computation.15 | async-start | bytes 2359296 | tf_op jit(solution)/shard_map/all_gather | solution.py:108
  213.6 51.1 %copy-start.17 = (f32[4,2048]{1,0:T(4,128)S(1)}, f32[4,2048]{1,0:T(4,128)}, u32[]{:S(2)}) copy-start(f32[4,2048]{1,0:T(4,128)} %param.23) | copy-start | bytes 98308
  215.0 56.7 %copy-start.10 = (bf16[1,16,2048]{2,1,0:T(8,128)(2,1)S(1)}, bf16[1,16,2048]{2,1,0:T(8,128)(2,1)}, u32[]{:S(2)}) copy-start(bf16[1,16,2048]{2,1,0:T(8,128)(2,1)} %param.12) | copy-start | bytes 196612
  259.9 11.6 %all-to-all-start.9 = ((bf16[4,16,2048]{2,1,0:T(8,128)(2,1)}), bf16[4,16,2048]{2,1,0:T(8,128)(2,1)S(1)}, u32[]{:S(2)}, u32[]{:S(2)}) async-start(bf16[4,16,2048]{2,1,0:T(8,128)(2,1)} %bitcast.38), calls=%async_computation.9 | async-start | bytes 524288 | tf_op jit(solution)/shard_map/all_to_all | solution.py:69
  294.6 26.9 %all-to-all-start.11 = ((bf16[4,128,2048]{2,1,0:T(8,128)(2,1)}), bf16[4,128,2048]{2,1,0:T(8,128)(2,1)S(1)}, u32[]{:S(2)}, u32[]{:S(2)}) async-start(bf16[4,128,2048]{2,1,0:T(8,128)(2,1)} %broadcast_in_dim.205), calls=%async_computation.11 | async-start | bytes 4194304 | tf_op jit(solution)/shard_map/all_to_all | solution.py:69
  298.3 25.2 %all-gather.5.cloned.1.call-start = ((), (), s32[]{:S(2)}) async-start(), calls=%async_computation.16 | async-start | bytes 1179648 | tf_op jit(solution)/shard_map/all_gather | solution.py:109
  328.6 30.7 %all-to-all-start.12 = ((bf16[4,128,2048]{2,1,0:T(8,128)(2,1)}), bf16[4,128,2048]{2,1,0:T(8,128)(2,1)S(1)}, u32[]{:S(2)}, u32[]{:S(2)}) async-start(bf16[4,128,2048]{2,1,0:T(8,128)(2,1)} %bitcast.116), calls=%async_computation.12 | async-start | bytes 4194304 | tf_op jit(solution)/shard_map/all_to_all | solution.py:69
  359.3 8.9 %all-to-all-start.14 = ((bf16[4,16,512]{2,1,0:T(8,128)(2,1)}), bf16[4,16,512]{2,1,0:T(8,128)(2,1)S(1)}, u32[]{:S(2)}, u32[]{:S(2)}) async-start(bf16[4,16,512]{2,1,0:T(8,128)(2,1)} %convert_element_type.166), calls=%async_computation.14 | async-start | bytes 131072 | tf_op jit(solution)/shard_map/all_to_all | solution.py:69
  368.2 22.6 %all-to-all-start.13 = ((bf16[8,16,2048]{2,1,0:T(8,128)(2,1)}), bf16[8,16,2048]{2,1,0:T(8,128)(2,1)S(1)}, u32[]{:S(2)}, u32[]{:S(2)}) async-start(bf16[8,16,2048]{2,1,0:T(8,128)(2,1)} %bitcast.47), calls=%async_computation.13 | async-start | bytes 1048576 | tf_op jit(solution)/shard_map/all_to_all | solution.py:69
Sparse Core Ops, SparseCore 0:
  213.4 28.6 all-gather.2
  300.9 22.2 all-gather.4
